TPU v7x, 256 devices: a whole 4x4x8 slice. The times are simulated.
256 devices in a mesh: sx: 8 (over z), sy: 32 (over y, x, core).
Axes of the slice: x: 4, y: 4, z: 8, core: 2. Of those that a mesh axis runs over, the one named last changes fastest.
Arguments:
- loads: float32 [12288, 4096], P('sx', 'sy'), may hold values from -6 to 6
- dual_op: bfloat16 [12288, 49152], P('sx', 'sy'), as said below
- dirichlet: bfloat16 [12288, 49152], P('sx', 'sy'), as said below
- corner_coupling: bfloat16 [128, 49152], P('sx', 'sy'), may hold values from -0.625 to 0.625
- corner_map: int32 [8, 512], P('sx', 'sy'), may hold values from 0 to 2047, as said below
- coarse_inverse: float32 [2048, 2048], P('sy'), as said below
Outputs:
- multipliers: float32 [12288, 4096], P('sx', 'sy')
- residual: float32 [12288, 4096], P('sx', 'sy')
Inputs may be any that keep to these rules, and one draw needn't show every extreme that they name: `corner_map`: every coarse unknown is named by exactly two entries over all subdomains. `dual_op`: each subdomain's block is symmetric positive definite. `dirichlet`: each subdomain's block is symmetric positive definite. `coarse_inverse`: symmetric positive definite.
All inputs are finite; a program needn't handle non-finite values.
Results may differ from a plain program's by a relative error of at most 0.014.
Values sent between devices are 32-bit elements; how exact they have to be, the bound alone decides.
No kernel may reach another device: no remote copies, remote signals or barrier semaphores. Data moves between devices by JAX's collectives and lax.ppermute only.
A program may use at most 64 MiB of HBM per device.

v0:
```python
import jax
import jax.numpy as jnp
from jax import lax
from jax.sharding import PartitionSpec as P

FACE = 320
EDGE = 64
ITERS = 4
HALF = 0.5
HIGH = lax.Precision.HIGHEST


def passed_along(value, axis, steps):
    count = lax.axis_size(axis)
    first, last = (max(0, -steps), min(count, count - steps))
    return lax.ppermute(value, axis, [(source, source + steps) for source in range(first, last)])


def padded(block, sides, width):
    for axis, dim in sides:
        count = lax.axis_size(axis)
        forward = [(i, i + 1) for i in range(count - 1)]
        backward = [(target, source) for source, target in forward]
        low = lax.ppermute(
            lax.slice_in_dim(block, block.shape[dim] - width, None, axis=dim), axis, forward
        )
        high = lax.ppermute(lax.slice_in_dim(block, 0, width, axis=dim), axis, backward)
        block = jnp.concatenate([low, block, high], axis=dim)
    return block


def split_blocks(field):
    widths = [FACE, FACE, FACE, FACE, EDGE, EDGE, EDGE, EDGE]
    pieces = []
    start = 0
    for width in widths:
        pieces.append(field[start : start + width])
        start = start + width
    return pieces


def assemble(field):
    pieces = split_blocks(field)
    upper_face = passed_along(pieces[1], "sx", 1)
    lower_face = passed_along(pieces[0], "sx", -1)
    left_face = passed_along(pieces[3], "sy", 1)
    right_face = passed_along(pieces[2], "sy", -1)
    stacked = jnp.concatenate([pieces[4], pieces[5], pieces[6], pieces[7]], axis=0)[None, None]
    bordered = padded(stacked, (("sx", 0), ("sy", 1)), 1)
    incoming = [
        upper_face,
        lower_face,
        left_face,
        right_face,
        bordered[0, 0, 3 * EDGE : 4 * EDGE],
        bordered[0, 2, 2 * EDGE : 3 * EDGE],
        bordered[2, 0, EDGE : 2 * EDGE],
        bordered[2, 2, 0:EDGE],
    ]
    return jnp.concatenate([mine + HALF * theirs for mine, theirs in zip(pieces, incoming)], axis=0)


def operate(direction, dual_op, corner_coupling, selector, coarse_inverse):
    spread = assemble(direction)
    rounded = spread.astype(jnp.bfloat16)
    local = jnp.dot(dual_op, rounded, preferred_element_type=jnp.float32)
    corner_part = jnp.dot(corner_coupling, rounded, preferred_element_type=jnp.float32)
    scattered = jnp.dot(selector.T, corner_part, precision=HIGH)
    coarse_sum = lax.psum(scattered, ("sx", "sy"))
    owned_rows = jnp.dot(coarse_inverse, coarse_sum, precision=HIGH)
    solution = lax.all_gather(owned_rows, "sy", axis=0, tiled=True)
    picked = jnp.dot(selector, solution, precision=HIGH)
    correction = jnp.dot(corner_coupling.astype(jnp.float32).T, picked, precision=HIGH)
    return assemble(local + correction)


def residual_norm(residual, smoothed):
    return lax.psum(jnp.sum(residual * smoothed, axis=0), ("sx", "sy"))


def body(loads, dual_op, dirichlet, corner_coupling, corner_map, coarse_inverse):
    corners = corner_map.shape[1]
    coarse_order = coarse_inverse.shape[1]
    selector = (
        corner_map[0][:, None] == lax.broadcasted_iota(jnp.int32, (corners, coarse_order), 1)
    ).astype(jnp.float32)

    def smooth(residual):
        return jnp.dot(dirichlet, residual.astype(jnp.bfloat16), preferred_element_type=jnp.float32)

    multipliers = jnp.zeros_like(loads)
    residual = loads
    smoothed = smooth(residual)
    direction = smoothed
    current = residual_norm(residual, smoothed)
    for step in range(ITERS):
        image = operate(direction, dual_op, corner_coupling, selector, coarse_inverse)
        alpha = current / lax.psum(jnp.sum(direction * image, axis=0), ("sx", "sy"))
        multipliers = multipliers + alpha * direction
        residual = residual - alpha * image
        if step + 1 < ITERS:
            smoothed = smooth(residual)
            following = residual_norm(residual, smoothed)
            direction = smoothed + following / current * direction
            current = following
    return (multipliers, residual)


def solution(mesh):
    in_specs = (
        P("sx", "sy"),
        P("sx", "sy"),
        P("sx", "sy"),
        P("sx", "sy"),
        P("sx", "sy"),
        P("sy", None),
    )
    out_specs = (P("sx", "sy"), P("sx", "sy"))
    return jax.shard_map(body, mesh=mesh, in_specs=in_specs, out_specs=out_specs, check_vma=False)
```

profile of v0, /device:TPU:1, one launch (start us, length us, event | category | flops | bytes accessed | tf_op | source)
XLA Modules:
  0.0 2106.7 jit_solution(1776008902199709787)
XLA Ops:
  7.2 4.0 fusion.7
  12.6 5.0 collective-permute-start.4
  17.6 3.6 collective-permute-start
  22.5 4.3 collective-permute-start.2
  28.8 3.6 collective-permute-start.6
  37.2 4.4 collective-permute-done.7
  43.7 265.5 %all-reduce.6.cloned.1.call-done = f32[2048,128]{1,0:T(8,128)} async-done(((f32[2048,128]{1,0:T(8,128)}), f32[2048,128]{1,0:T(8,128)}) %all-reduce.6.cloned.1.call-update) | async-done | bytes 1048592 | tf_op jit(solution)/shard_map/psum | solution.py:69
  309.2 2.6 convolution_bitcast_fusion.6
  311.9 3.7 fusion.122
  315.6 45.0 %all-gather.5.cloned.1.call-done = f32[2048,128]{1,0:T(8,128)} async-done(((f32[64,128]{1,0:T(8,128)}), f32[2048,128]{1,0:T(8,128)}) %all-gather.5.cloned.1.call-update) | async-done | bytes 1048592 | tf_op jit(solution)/shard_map/all_gather | solution.py:71
  362.9 3.2 collective-permute-start.8
  367.4 4.0 collective-permute-start.12
  373.4 4.5 collective-permute-start.14
  379.7 3.6 collective-permute-start.10
  385.7 4.4 collective-permute-done.11
  391.3 82.7 %all-reduce = (f32[128]{0:T(128)S(1)}, f32[128]{0:T(128)S(1)}) all-reduce(f32[128]{0:T(128)S(1)} %get-tuple-element.3, f32[128]{0:T(128)S(1)} %get-tuple-element.2), channel_id=1, replica_groups=mesh['sx'=8,'sy'=32] {'sx','sy'}, use_global_device_ids=true, to_apply=%region_1.0 | all-reduce | flops 256 | bytes 2048 | tf_op jit(solution)/shard_map/psum | solution.py:78
  475.3 4.6 multiply_reduce_fusion.5
  479.9 74.7 %psum.87 = f32[128]{0:T(128)S(1)} all-reduce(f32[128]{0:T(128)S(1)} %get-tuple-element.40), channel_id=1, replica_groups=mesh['sx'=8,'sy'=32] {'sx','sy'}, use_global_device_ids=true, to_apply=%region_6.0 | all-reduce | flops 128 | bytes 1024 | tf_op jit(solution)/shard_map/psum | solution.py:78
  557.1 4.0 collective-permute-start.20
  564.4 4.1 collective-permute-start.18
  570.5 3.6 collective-permute-start.22
  578.8 4.4 collective-permute-done.23
  585.6 263.1 %all-reduce.8.cloned.1.call-done = f32[2048,128]{1,0:T(8,128)} async-done(((f32[2048,128]{1,0:T(8,128)}), f32[2048,128]{1,0:T(8,128)}) %all-reduce.8.cloned.1.call-update) | async-done | bytes 1048592 | tf_op jit(solution)/shard_map/psum | solution.py:69
  848.7 2.6 convolution_bitcast_fusion.5
  851.3 4.6 fusion.123
  856.0 44.0 %all-gather.7.cloned.1.call-done = f32[2048,128]{1,0:T(8,128)} async-done(((f32[64,128]{1,0:T(8,128)}), f32[2048,128]{1,0:T(8,128)}) %all-gather.7.cloned.1.call-update) | async-done | bytes 1048592 | tf_op jit(solution)/shard_map/all_gather | solution.py:71
  903.3 3.2 collective-permute-start.24
  907.8 4.0 collective-permute-start.28
  913.8 4.5 collective-permute-start.30
  920.2 3.6 collective-permute-start.26
  926.1 4.4 collective-permute-done.27
  931.7 82.7 %psum.89 = f32[128]{0:T(128)S(1)} all-reduce(f32[128]{0:T(128)S(1)} %multiply_reduce_fusion.4), channel_id=1, replica_groups=mesh['sx'=8,'sy'=32] {'sx','sy'}, use_global_device_ids=true, to_apply=%region_9.0 | all-reduce | flops 128 | bytes 1024 | tf_op jit(solution)/shard_map/psum | solution.py:98
  1016.5 4.6 multiply_reduce_fusion.3
  1021.2 74.7 %psum.90 = f32[128]{0:T(128)S(1)} all-reduce(f32[128]{0:T(128)S(1)} %get-tuple-element.42), channel_id=1, replica_groups=mesh['sx'=8,'sy'=32] {'sx','sy'}, use_global_device_ids=true, to_apply=%region_11.0 | all-reduce | flops 128 | bytes 1024 | tf_op jit(solution)/shard_map/psum | solution.py:78
  1098.4 4.0 collective-permute-start.36
  1105.7 4.1 collective-permute-start.34
  1111.7 3.6 collective-permute-start.38
  1120.1 4.4 collective-permute-done.39
  1126.6 263.3 %all-reduce.10.cloned.1.call-done = f32[2048,128]{1,0:T(8,128)} async-done(((f32[2048,128]{1,0:T(8,128)}), f32[2048,128]{1,0:T(8,128)}) %all-reduce.10.cloned.1.call-update) | async-done | bytes 1048592 | tf_op jit(solution)/shard_map/psum | solution.py:69
  1389.9 2.6 convolution_bitcast_fusion.4
  1392.6 4.6 fusion.124
  1397.2 43.7 %all-gather.9.cloned.1.call-done = f32[2048,128]{1,0:T(8,128)} async-done(((f32[64,128]{1,0:T(8,128)}), f32[2048,128]{1,0:T(8,128)}) %all-gather.9.cloned.1.call-update) | async-done | bytes 1048592 | tf_op jit(solution)/shard_map/all_gather | solution.py:71
  1444.4 3.2 collective-permute-start.40
  1448.9 4.0 collective-permute-start.44
  1454.8 4.5 collective-permute-start.46
  1461.2 3.6 collective-permute-start.42
  1467.1 4.4 collective-permute-done.43
  1472.7 82.7 %psum.92 = f32[128]{0:T(128)S(1)} all-reduce(f32[128]{0:T(128)S(1)} %multiply_reduce_fusion.2), channel_id=1, replica_groups=mesh['sx'=8,'sy'=32] {'sx','sy'}, use_global_device_ids=true, to_apply=%region_14.0 | all-reduce | flops 128 | bytes 1024 | tf_op jit(solution)/shard_map/psum | solution.py:98
  1557.8 4.6 multiply_reduce_fusion.1
  1562.4 74.8 %psum.93 = f32[128]{0:T(128)S(1)} all-reduce(f32[128]{0:T(128)S(1)} %get-tuple-element.44), channel_id=1, replica_groups=mesh['sx'=8,'sy'=32] {'sx','sy'}, use_global_device_ids=true, to_apply=%region_16.0 | all-reduce | flops 128 | bytes 1024 | tf_op jit(solution)/shard_map/psum | solution.py:78
  1639.8 4.0 collective-permute-start.52
  1647.1 3.9 collective-permute-start.50
  1653.0 3.6 collective-permute-start.54
  1661.4 4.4 collective-permute-done.55
  1667.9 263.3 %all-reduce.12.cloned.1.call-done = f32[2048,128]{1,0:T(8,128)} async-done(((f32[2048,128]{1,0:T(8,128)}), f32[2048,128]{1,0:T(8,128)}) %all-reduce.12.cloned.1.call-update) | async-done | bytes 1048592 | tf_op jit(solution)/shard_map/psum | solution.py:69
  1933.9 4.6 fusion.125
  1938.5 43.8 %all-gather.11.cloned.1.call-done = f32[2048,128]{1,0:T(8,128)} async-done(((f32[64,128]{1,0:T(8,128)}), f32[2048,128]{1,0:T(8,128)}) %all-gather.11.cloned.1.call-update) | async-done | bytes 1048592 | tf_op jit(solution)/shard_map/all_gather | solution.py:71
  1985.8 3.2 collective-permute-start.56
  1990.3 4.0 collective-permute-start.60
  1996.2 4.5 collective-permute-start.62
  2002.6 3.6 collective-permute-start.58
  2008.5 4.4 collective-permute-done.59
  2014.1 82.7 %psum.95 = f32[128]{0:T(128)S(1)} all-reduce(f32[128]{0:T(128)S(1)} %multiply_reduce_fusion), channel_id=1, replica_groups=mesh['sx'=8,'sy'=32] {'sx','sy'}, use_global_device_ids=true, to_apply=%region_19.0 | all-reduce | flops 128 | bytes 1024 | tf_op jit(solution)/shard_map/psum | solution.py:98
  2096.9 3.0 multiply_subtract_fusion
  (253 shorter events, 110.5 us)
Async XLA Ops:
  7.2 302.0 %all-reduce.6.cloned.1.call-start = ((), (), s32[]{:S(2)}) async-start(), calls=%async_computation | async-start | bytes 2097152 | tf_op jit(solution)/shard_map/psum | solution.py:69
  11.3 15.6 collective-permute-start.5
  12.6 16.2 collective-permute-start.4
  17.6 14.8 collective-permute-start
  21.2 13.3 collective-permute-start.1
  22.5 12.0 collective-permute-start.2
  26.8 7.7 collective-permute-start.3
  28.8 8.3 collective-permute-start.6
  32.5 9.1 collective-permute-start.7
  43.7 316.9 %all-gather.5.cloned.1.call-start = ((), (), s32[]{:S(2)}) async-start(), calls=%async_computation.1 | async-start | bytes 1081344 | tf_op jit(solution)/shard_map/all_gather | solution.py:71
  311.8 536.8 %all-reduce.8.cloned.1.call-start = ((), (), s32[]{:S(2)}) async-start(), calls=%async_computation.2 | async-start | bytes 2097152 | tf_op jit(solution)/shard_map/psum | solution.py:69
  362.9 8.5 collective-permute-start.8
  366.1 6.7 collective-permute-start.13
  371.5 13.9 collective-permute-start.9
  373.4 16.7 collective-permute-start.14
  377.8 12.3 collective-permute-start.15
  383.4 6.6 collective-permute-start.11
  555.8 12.7 collective-permute-start.21
  557.1 13.3 collective-permute-start.20
  561.2 13.0 collective-permute-start.16
  563.1 13.0 collective-permute-start.17
  564.4 11.7 collective-permute-start.18
  568.5 7.7 collective-permute-start.19
  570.5 8.3 collective-permute-start.22
  574.1 9.1 collective-permute-start.23
  585.3 314.6 %all-gather.7.cloned.1.call-start = ((), (), s32[]{:S(2)}) async-start(), calls=%async_computation.3 | async-start | bytes 1081344 | tf_op jit(solution)/shard_map/all_gather | solution.py:71
  851.3 538.6 %all-reduce.10.cloned.1.call-start = ((), (), s32[]{:S(2)}) async-start(), calls=%async_computation.4 | async-start | bytes 2097152 | tf_op jit(solution)/shard_map/psum | solution.py:69
  903.3 8.5 collective-permute-start.24
  906.5 6.7 collective-permute-start.29
  911.9 13.9 collective-permute-start.25
  913.8 16.7 collective-permute-start.30
  918.3 12.3 collective-permute-start.31
  923.8 6.6 collective-permute-start.27
  1097.1 12.7 collective-permute-start.37
  1098.4 13.3 collective-permute-start.36
  1102.4 13.0 collective-permute-start.32
  1104.4 13.0 collective-permute-start.33
  1105.7 11.7 collective-permute-start.34
  1109.8 7.7 collective-permute-start.35
  1111.7 8.3 collective-permute-start.38
  1115.4 9.1 collective-permute-start.39
  1126.6 314.4 %all-gather.9.cloned.1.call-start = ((), (), s32[]{:S(2)}) async-start(), calls=%async_computation.5 | async-start | bytes 1081344 | tf_op jit(solution)/shard_map/all_gather | solution.py:71
  1392.6 538.7 %all-reduce.12.cloned.1.call-start = ((), (), s32[]{:S(2)}) async-start(), calls=%async_computation.6 | async-start | bytes 2097152 | tf_op jit(solution)/shard_map/psum | solution.py:69
  1444.4 8.5 collective-permute-start.40
  1447.6 6.7 collective-permute-start.45
  1452.9 14.1 collective-permute-start.41
  1454.8 16.7 collective-permute-start.46
  1459.3 12.3 collective-permute-start.47
  1464.9 6.6 collective-permute-start.43
  1638.5 12.5 collective-permute-start.53
  1639.8 13.2 collective-permute-start.52
  1643.8 12.8 collective-permute-start.48
  1645.8 12.9 collective-permute-start.49
  1647.1 11.6 collective-permute-start.50
  1651.0 7.7 collective-permute-start.51
  1653.0 8.3 collective-permute-start.54
  1656.7 9.1 collective-permute-start.55
  1667.9 314.4 %all-gather.11.cloned.1.call-start = ((), (), s32[]{:S(2)}) async-start(), calls=%async_computation.7 | async-start | bytes 1081344 | tf_op jit(solution)/shard_map/all_gather | solution.py:71
  1985.8 8.5 collective-permute-start.56
  1989.0 6.7 collective-permute-start.61
  1994.3 13.9 collective-permute-start.57
  1996.2 16.7 collective-permute-start.62
  2000.7 12.3 collective-permute-start.63
  2006.3 6.6 collective-permute-start.59
  (20 other events, 558.1 us)
Sparse Core Ops, SparseCore 0:
  43.8 265.3 all-reduce.5
  312.3 48.2 all-gather.4
  585.4 263.1 all-reduce.7
  851.6 48.2 all-gather.6
  1126.7 263.1 all-reduce.9
  1392.7 48.2 all-gather.8
  1668.0 263.2 all-reduce.11
  1934.0 48.2 all-gather.10
where the time goes:
time: 2110 us
  waiting for transfers between devices  1280 us (61%)
  blocking collectives  555 us (26%)
  starting transfers between devices  171 us (8%)
  matrix products  66.4 us (3%)
    psum x4, waiting for transfers between devices, operate(): coarse_sum = lax.psum(scattered, ('sx', 'sy'))  1060 us
    psum x4, blocking collectives, residual_norm(): return lax.psum(jnp.sum(residual * smoothed, axis=0), ('sx', 'sy'))  307 us
    psum x3, blocking collectives, body(): alpha = current / lax.psum(jnp.sum(direction * image, axis=0), ('sx', 'sy'))  248 us
    all_gather x4, waiting for transfers between devices, operate(): solution = lax.all_gather(owned_rows, 'sy', axis=0, tiled=True)  176 us
    ppermute x32, starting transfers between devices, passed_along(): lax.ppermute(value, axis, [(source, source + steps) for source in range(f...  79 us
    ppermute x16, starting transfers between devices, padded(): lax.ppermute(lax.slice_in_dim(block, block.shape[dim] - width, None, axis...  65.3 us
  transfers between devices with their start and end apart: 72, of which 28 were waited for; matrix products, arithmetic and copies ran while one was open for 1% of the time, Pallas kernels for 0%

commit v1 on v0

--- a/solution.py
+++ b/solution.py
@@ -8,6 +8,13 @@
 ITERS = 4
 HALF = 0.5
 HIGH = lax.Precision.HIGHEST
+
+
+def swapped_in(value, mesh_axis, along):
+    size = lax.axis_size(mesh_axis)
+    parts = jnp.stack([value for _ in range(size)])
+    parts = lax.all_to_all(parts, mesh_axis, split_axis=0, concat_axis=0)
+    return jnp.concatenate(parts, axis=along)
 
 
 def passed_along(value, axis, steps):
@@ -68,7 +75,7 @@
     scattered = jnp.dot(selector.T, corner_part, precision=HIGH)
     coarse_sum = lax.psum(scattered, ("sx", "sy"))
     owned_rows = jnp.dot(coarse_inverse, coarse_sum, precision=HIGH)
-    solution = lax.all_gather(owned_rows, "sy", axis=0, tiled=True)
+    solution = swapped_in(owned_rows, "sy", 0)
     picked = jnp.dot(selector, solution, precision=HIGH)
     correction = jnp.dot(corner_coupling.astype(jnp.float32).T, picked, precision=HIGH)
     return assemble(local + correction)

time: 2110 us -> 2020 us (0.957)
  waiting for transfers between devices: 1280 us -> 1150 us
  starting transfers between devices: 171 us -> 203 us
    all_gather x4 -> x0, waiting for transfers between devices: 176 us -> none  [operate(): solution = lax.all_gather(owned_rows, 'sy', axis=0, tiled=True)]
    all_to_all x0 -> x4, waiting for transfers between devices: none -> 40.1 us  [swapped_in(): parts = lax.all_to_all(parts, mesh_axis, split_axis=0, concat_axis=0)]
    all_to_all x0 -> x4, starting transfers between devices: none -> 34.1 us  [swapped_in(): parts = lax.all_to_all(parts, mesh_axis, split_axis=0, concat_axis=0)]
where the time goes in v1:
time: 2020 us; the launch traced here: 2010 us
  waiting for transfers between devices  1150 us (57%)
  blocking collectives  553 us (27%)
  starting transfers between devices  203 us (10%)
  matrix products  65 us (3%)
    psum x4, waiting for transfers between devices, operate(): coarse_sum = lax.psum(scattered, ('sx', 'sy'))  1060 us
    psum x4, blocking collectives, residual_norm(): return lax.psum(jnp.sum(residual * smoothed, axis=0), ('sx', 'sy'))  307 us
    psum x3, blocking collectives, body(): alpha = current / lax.psum(jnp.sum(direction * image, axis=0), ('sx', 'sy'))  246 us
    ppermute x32, starting transfers between devices, passed_along(): lax.ppermute(value, axis, [(source, source + steps) for source in range(f...  70.6 us
    ppermute x16, starting transfers between devices, padded(): lax.ppermute(lax.slice_in_dim(block, block.shape[dim] - width, None, axis...  62.7 us
  transfers between devices with their start and end apart: 72, of which 28 were waited for; matrix products, arithmetic and copies ran while one was open for 1% of the time, Pallas kernels for 0%

profile of v1, /device:TPU:1, one launch (start us, length us, event | category | flops | bytes accessed | tf_op | source)
XLA Modules:
  0.0 2007.0 jit_solution(16078455720477667792)
XLA Ops:
  7.2 4.0 fusion.7
  12.6 5.0 collective-permute-start.4
  17.6 3.5 collective-permute-start
  22.5 4.3 collective-permute-start.2
  28.8 3.6 collective-permute-start.6
  34.6 2.6 collective-permute-done.6
  37.2 4.4 collective-permute-done.7
  43.7 265.7 %all-reduce.6.cloned.1.call-done = f32[2048,128]{1,0:T(8,128)} async-done(((f32[2048,128]{1,0:T(8,128)}), f32[2048,128]{1,0:T(8,128)}) %all-reduce.6.cloned.1.call-update) | async-done | bytes 1048592 | tf_op jit(solution)/shard_map/psum | solution.py:76
  312.5 8.5 all-to-all-start
  321.0 4.6 fusion.122
  325.6 12.4 all-to-all-done
  342.8 4.0 collective-permute-start.12
  349.0 3.8 collective-permute-start.14
  354.7 3.6 collective-permute-start.10
  360.7 4.4 collective-permute-done.11
  366.3 81.9 %all-reduce = (f32[128]{0:T(128)S(1)}, f32[128]{0:T(128)S(1)}) all-reduce(f32[128]{0:T(128)S(1)} %get-tuple-element.3, f32[128]{0:T(128)S(1)} %get-tuple-element.2), channel_id=1, replica_groups=mesh['sx'=8,'sy'=32] {'sx','sy'}, use_global_device_ids=true, to_apply=%region_1.0 | all-reduce | flops 256 | bytes 2048 | tf_op jit(solution)/shard_map/psum | solution.py:85
  449.4 4.6 multiply_reduce_fusion.5
  454.0 75.1 %psum.87 = f32[128]{0:T(128)S(1)} all-reduce(f32[128]{0:T(128)S(1)} %get-tuple-element.40), channel_id=1, replica_groups=mesh['sx'=8,'sy'=32] {'sx','sy'}, use_global_device_ids=true, to_apply=%region_6.0 | all-reduce | flops 128 | bytes 1024 | tf_op jit(solution)/shard_map/psum | solution.py:85
  531.7 4.0 collective-permute-start.20
  539.0 3.9 collective-permute-start.18
  544.9 3.6 collective-permute-start.22
  553.2 4.4 collective-permute-done.23
  560.5 263.4 %all-reduce.8.cloned.1.call-done = f32[2048,128]{1,0:T(8,128)} async-done(((f32[2048,128]{1,0:T(8,128)}), f32[2048,128]{1,0:T(8,128)}) %all-reduce.8.cloned.1.call-update) | async-done | bytes 1048592 | tf_op jit(solution)/shard_map/psum | solution.py:76
  827.0 8.5 all-to-all-start.1
  835.6 4.7 fusion.123
  840.3 12.4 all-to-all-done.1
  858.7 4.0 collective-permute-start.28
  864.8 3.8 collective-permute-start.30
  870.6 3.6 collective-permute-start.26
  876.5 4.4 collective-permute-done.27
  882.1 81.9 %psum.89 = f32[128]{0:T(128)S(1)} all-reduce(f32[128]{0:T(128)S(1)} %multiply_reduce_fusion.4), channel_id=1, replica_groups=mesh['sx'=8,'sy'=32] {'sx','sy'}, use_global_device_ids=true, to_apply=%region_9.0 | all-reduce | flops 128 | bytes 1024 | tf_op jit(solution)/shard_map/psum | solution.py:105
  966.0 4.6 multiply_reduce_fusion.3
  970.7 75.2 %psum.90 = f32[128]{0:T(128)S(1)} all-reduce(f32[128]{0:T(128)S(1)} %get-tuple-element.42), channel_id=1, replica_groups=mesh['sx'=8,'sy'=32] {'sx','sy'}, use_global_device_ids=true, to_apply=%region_11.0 | all-reduce | flops 128 | bytes 1024 | tf_op jit(solution)/shard_map/psum | solution.py:85
  1048.5 4.0 collective-permute-start.36
  1055.7 3.8 collective-permute-start.34
  1061.5 3.6 collective-permute-start.38
  1067.3 2.6 collective-permute-done.38
  1069.9 4.4 collective-permute-done.39
  1077.2 263.3 %all-reduce.10.cloned.1.call-done = f32[2048,128]{1,0:T(8,128)} async-done(((f32[2048,128]{1,0:T(8,128)}), f32[2048,128]{1,0:T(8,128)}) %all-reduce.10.cloned.1.call-update) | async-done | bytes 1048592 | tf_op jit(solution)/shard_map/psum | solution.py:76
  1343.6 8.5 all-to-all-start.2
  1352.1 9.4 all-reduce.12.cloned.1.call-start
  1361.6 4.7 fusion.124
  1366.3 3.0 all-to-all-done.2
  1375.3 4.0 collective-permute-start.44
  1381.5 3.8 collective-permute-start.46
  1387.2 3.6 collective-permute-start.42
  1393.1 4.4 collective-permute-done.43
  1398.7 81.9 %psum.92 = f32[128]{0:T(128)S(1)} all-reduce(f32[128]{0:T(128)S(1)} %multiply_reduce_fusion.2), channel_id=1, replica_groups=mesh['sx'=8,'sy'=32] {'sx','sy'}, use_global_device_ids=true, to_apply=%region_14.0 | all-reduce | flops 128 | bytes 1024 | tf_op jit(solution)/shard_map/psum | solution.py:105
  1482.9 4.6 multiply_reduce_fusion.1
  1487.5 75.2 %psum.93 = f32[128]{0:T(128)S(1)} all-reduce(f32[128]{0:T(128)S(1)} %get-tuple-element.44), channel_id=1, replica_groups=mesh['sx'=8,'sy'=32] {'sx','sy'}, use_global_device_ids=true, to_apply=%region_16.0 | all-reduce | flops 128 | bytes 1024 | tf_op jit(solution)/shard_map/psum | solution.py:85
  1565.3 4.0 collective-permute-start.52
  1572.6 3.8 collective-permute-start.50
  1578.4 3.6 collective-permute-start.54
  1586.7 4.4 collective-permute-done.55
  1594.0 263.3 %all-reduce.12.cloned.1.call-done = f32[2048,128]{1,0:T(8,128)} async-done(((f32[2048,128]{1,0:T(8,128)}), f32[2048,128]{1,0:T(8,128)}) %all-reduce.12.cloned.1.call-update) | async-done | bytes 1048592 | tf_op jit(solution)/shard_map/psum | solution.py:76
  1860.4 8.5 all-to-all-start.3
  1869.0 4.7 fusion.125
  1873.7 12.4 all-to-all-done.3
  1892.2 4.0 collective-permute-start.60
  1898.4 3.8 collective-permute-start.62
  1904.1 3.6 collective-permute-start.58
  1910.0 4.4 collective-permute-done.59
  1915.6 81.9 %psum.95 = f32[128]{0:T(128)S(1)} all-reduce(f32[128]{0:T(128)S(1)} %multiply_reduce_fusion), channel_id=1, replica_groups=mesh['sx'=8,'sy'=32] {'sx','sy'}, use_global_device_ids=true, to_apply=%region_19.0 | all-reduce | flops 128 | bytes 1024 | tf_op jit(solution)/shard_map/psum | solution.py:105
  1997.5 3.0 multiply_subtract_fusion
  (259 shorter events, 122.9 us)
Async XLA Ops:
  7.2 302.1 %all-reduce.6.cloned.1.call-start = ((), (), s32[]{:S(2)}) async-start(), calls=%async_computation.4 | async-start | bytes 2097152 | tf_op jit(solution)/shard_map/psum | solution.py:76
  11.3 15.6 collective-permute-start.5
  12.6 16.2 collective-permute-start.4
  17.6 14.8 collective-permute-start
  21.2 13.3 collective-permute-start.1
  22.5 12.0 collective-permute-start.2
  26.8 7.7 collective-permute-start.3
  28.8 8.3 collective-permute-start.6
  32.5 9.1 collective-permute-start.7
  312.5 25.5 %all-to-all-start = ((f32[32,64,128]{2,1,0:T(8,128)}), f32[32,64,128]{2,1,0:T(8,128)S(1)}, u32[]{:S(2)}, u32[]{:S(2)}) async-start(f32[32,64,128]{2,1,0:T(8,128)} %stack.8), calls=%async_computation | async-start | bytes 2097152 | tf_op jit(solution)/shard_map/all_to_all | solution.py:16
  321.0 502.9 %all-reduce.8.cloned.1.call-start = ((), (), s32[]{:S(2)}) async-start(), calls=%async_computation.5 | async-start | bytes 2097152 | tf_op jit(solution)/shard_map/psum | solution.py:76
  340.2 6.6 collective-permute-start.8
  341.5 6.7 collective-permute-start.13
  346.9 13.4 collective-permute-start.9
  349.0 16.0 collective-permute-start.14
  352.8 12.3 collective-permute-start.15
  358.4 6.6 collective-permute-start.11
  530.4 12.5 collective-permute-start.21
  531.7 13.1 collective-permute-start.20
  535.7 12.8 collective-permute-start.16
  537.7 13.1 collective-permute-start.17
  539.0 11.9 collective-permute-start.18
  542.9 8.0 collective-permute-start.19
  544.9 8.3 collective-permute-start.22
  548.5 9.1 collective-permute-start.23
  827.0 25.6 %all-to-all-start.1 = ((f32[32,64,128]{2,1,0:T(8,128)}), f32[32,64,128]{2,1,0:T(8,128)}, u32[]{:S(2)}, u32[]{:S(2)}) async-start(f32[32,64,128]{2,1,0:T(8,128)} %stack.9), calls=%async_computation.1 | async-start | bytes 2097152 | tf_op jit(solution)/shard_map/all_to_all | solution.py:16
  835.5 505.0 %all-reduce.10.cloned.1.call-start = ((), (), s32[]{:S(2)}) async-start(), calls=%async_computation.6 | async-start | bytes 2097152 | tf_op jit(solution)/shard_map/psum | solution.py:76
  856.0 6.6 collective-permute-start.24
  857.4 6.7 collective-permute-start.29
  862.7 13.4 collective-permute-start.25
  864.8 16.0 collective-permute-start.30
  868.6 12.3 collective-permute-start.31
  874.2 6.6 collective-permute-start.27
  1047.2 12.4 collective-permute-start.37
  1048.5 13.0 collective-permute-start.36
  1052.5 12.7 collective-permute-start.32
  1054.4 12.7 collective-permute-start.33
  1055.7 11.4 collective-permute-start.34
  1059.5 7.7 collective-permute-start.35
  1061.5 8.3 collective-permute-start.38
  1065.2 9.1 collective-permute-start.39
  1343.6 25.6 %all-to-all-start.2 = ((f32[32,64,128]{2,1,0:T(8,128)}), f32[32,64,128]{2,1,0:T(8,128)}, u32[]{:S(2)}, u32[]{:S(2)}) async-start(f32[32,64,128]{2,1,0:T(8,128)} %stack.10), calls=%async_computation.2 | async-start | bytes 2097152 | tf_op jit(solution)/shard_map/all_to_all | solution.py:16
  1352.1 505.2 %all-reduce.12.cloned.1.call-start = ((), (), s32[]{:S(2)}) async-start(), calls=%async_computation.7 | async-start | bytes 2097152 | tf_op jit(solution)/shard_map/psum | solution.py:76
  1372.6 6.6 collective-permute-start.40
  1374.0 6.7 collective-permute-start.45
  1379.3 13.4 collective-permute-start.41
  1381.5 16.0 collective-permute-start.46
  1385.2 12.3 collective-permute-start.47
  1390.8 6.6 collective-permute-start.43
  1564.0 12.4 collective-permute-start.53
  1565.3 13.0 collective-permute-start.52
  1569.4 12.7 collective-permute-start.48
  1571.3 12.7 collective-permute-start.49
  1572.6 11.4 collective-permute-start.50
  1576.4 7.7 collective-permute-start.51
  1578.4 8.3 collective-permute-start.54
  1582.0 9.1 collective-permute-start.55
  1860.4 25.6 %all-to-all-start.3 = ((f32[32,64,128]{2,1,0:T(8,128)}), f32[32,64,128]{2,1,0:T(8,128)}, u32[]{:S(2)}, u32[]{:S(2)}) async-start(f32[32,64,128]{2,1,0:T(8,128)} %stack.11), calls=%async_computation.3 | async-start | bytes 2097152 | tf_op jit(solution)/shard_map/all_to_all | solution.py:16
  1889.6 6.6 collective-permute-start.56
  1890.9 6.7 collective-permute-start.61
  1896.3 13.4 collective-permute-start.57
  1898.4 16.0 collective-permute-start.62
  1902.2 12.3 collective-permute-start.63
  1907.8 6.6 collective-permute-start.59
  (23 other events, 524.0 us)
Sparse Core Ops, SparseCore 0:
  43.8 265.4 all-reduce.5
  560.6 263.2 all-reduce.7
  1077.3 263.1 all-reduce.9
  1594.1 263.1 all-reduce.11
